TPU v7x, 128 devices: a whole 4x4x4 slice. The times are simulated.
128 devices in a mesh: row: 4 (over y_lo, core), col: 32 (over z, y_hi, x).
Axes of the slice: x: 4, y: 4 (y_hi: 2, y_lo: 2; y = y_hi * 2 + y_lo), z: 4, core: 2. Of those that a mesh axis runs over, the one named last changes fastest.
Arguments:
- orbitals: bfloat16 [256, 8, 48, 2304], P(('row', 'col')), may hold values from -6 to 6
- potential_boxes: float32 [256, 48, 2304], P(('row', 'col')), may hold values from 0 to 2
- corners: int32 [256, 3], P(('row', 'col')), may hold values from 0 to 511, as said below
- signs: int32 [256], P(('row', 'col')), may hold values from -1 to 1, as said below
- counts: int32 [256], P(('row', 'col')), may hold values from 1 to 8, as said below
Outputs:
- filtered: bfloat16 [256, 8, 48, 2304], P(('row', 'col'))
- density: float32 [64, 256, 512], P('row', 'col')
- hartree: float32 [64, 256, 512], P('row', 'col')
Inputs may be any that keep to these rules, and one draw needn't show every extreme that they name: `corners`: for fragment f held at index d = f // 2 of the row+col axis, with r = d // 32 and c = d % 32, the corner's first entry lies in [r * 16, (r + 1) * 16) and its second in [c * 8, (c + 1) * 8); the third is any cell below 512. Fragments 2 i and 2 i + 1 have the same corner. Each entry is -1 or 1; fragments 2 i and 2 i + 1 have opposite signs. Fragments 2 i and 2 i + 1 have equal counts; some device holds a fragment with 8 and some device one with 1.
All inputs are finite; a program needn't handle non-finite values.
Results may differ from a plain program's by a relative error of at most 0.001.
Values may be sent and summed in bfloat16 or wider, within the bound.
No kernel may reach another device: no remote copies, remote signals or barrier semaphores. Data moves between devices by JAX's collectives and lax.ppermute only.
A program may use at most 128 MiB of HBM per device.

v0:
```python
import math

import jax
import jax.numpy as jnp
from jax import lax
from jax.sharding import PartitionSpec as P

B = 48
DEGREE = 6
CX = 16
CY = 8
NZ = 512


CENTER = 5.25
HALF_WIDTH = 3.75
SCREEN = 0.0025
HIGHEST = lax.Precision.HIGHEST


def passed_along(value, axis, by):
    peers = lax.axis_size(axis)
    return lax.ppermute(value, axis, [(i, (i + by) % peers) for i in range(peers)])


def hamiltonian(field, potential):
    side = field.shape[0]
    zpos = lax.broadcasted_iota(jnp.int32, field.shape, 1) % side
    zero_row = jnp.zeros_like(field[:1])
    next_x = jnp.concatenate([field[1:], zero_row], 0)
    prev_x = jnp.concatenate([zero_row, field[:-1]], 0)
    zero_col = jnp.zeros_like(field[:, :1])
    next_z = jnp.concatenate([field[:, 1:], zero_col], 1)
    prev_z = jnp.concatenate([zero_col, field[:, :-1]], 1)
    next_z = jnp.where(zpos == side - 1, 0.0, next_z)
    prev_z = jnp.where(zpos == 0, 0.0, prev_z)
    zero_plane = jnp.zeros_like(field[:, :side])
    next_y = jnp.concatenate([field[:, side:], zero_plane], 1)
    prev_y = jnp.concatenate([zero_plane, field[:, :-side]], 1)
    beside = next_x + prev_x + next_z + prev_z + next_y + prev_y
    return (3.0 + potential) * field - 0.5 * beside


def chebyshev(start, potential):

    def shifted(field):
        return (hamiltonian(field, potential) - CENTER * field) / HALF_WIDTH

    previous = start
    current = shifted(start)
    for order in range(2, DEGREE + 1):
        previous, current = (current, 2.0 * shifted(current) - previous)
    scale = lax.rsqrt(jnp.mean(current * current) + 1e-06)
    return current * scale


def filter_fragment(orbital_set, potential, live_count):

    def advance(index, carry):
        result, box_density = carry
        single = lax.dynamic_index_in_dim(orbital_set, index, 0, keepdims=False).astype(jnp.float32)
        smooth = chebyshev(single, potential)
        result = lax.dynamic_update_index_in_dim(result, smooth.astype(jnp.bfloat16), index, 0)
        return (result, box_density + smooth * smooth)

    initial = (jnp.zeros(orbital_set.shape, jnp.bfloat16), jnp.zeros(potential.shape, jnp.float32))
    return lax.fori_loop(0, live_count, advance, initial)


def place_all(slab, cubes, offsets, lift):
    start = (offsets[0, 1] + lift, offsets[0, 0], offsets[0, 2])
    slab = lax.dynamic_update_slice(slab, jnp.transpose(cubes[0], (1, 0, 2)), start)
    return slab


def wrap_depth(slab):
    head = slab[:, :, :NZ]
    return head.at[:, :, :B].add(slab[:, :, NZ:])


def wave_square(length, positions):
    signed_index = jnp.where(positions <= length // 2, positions, positions - length).astype(
        jnp.float32
    )
    wave = signed_index * (2 * math.pi / length)
    return wave * wave


def tables(length):
    product = (
        lax.broadcasted_iota(jnp.int32, (length, length), 0)
        * lax.broadcasted_iota(jnp.int32, (length, length), 1)
        % length
    )
    angle = product.astype(jnp.float32) * (2 * math.pi / length)
    return (jnp.cos(angle), jnp.sin(angle))


def along_last(real_part, imag_part, cosines, sines, sign):
    real_cos = jnp.einsum("abn,nk->abk", real_part, cosines, precision=HIGHEST)
    real_sin = jnp.einsum("abn,nk->abk", real_part, sines, precision=HIGHEST)
    imag_cos = jnp.einsum("abn,nk->abk", imag_part, cosines, precision=HIGHEST)
    imag_sin = jnp.einsum("abn,nk->abk", imag_part, sines, precision=HIGHEST)
    return (real_cos - sign * imag_sin, imag_cos + sign * real_sin)


def along_first(real_part, imag_part, cosines, sines, sign):
    real_cos = jnp.einsum("nab,nk->kab", real_part, cosines, precision=HIGHEST)
    real_sin = jnp.einsum("nab,nk->kab", real_part, sines, precision=HIGHEST)
    imag_cos = jnp.einsum("nab,nk->kab", imag_part, cosines, precision=HIGHEST)
    imag_sin = jnp.einsum("nab,nk->kab", imag_part, sines, precision=HIGHEST)
    return (real_cos - sign * imag_sin, imag_cos + sign * real_sin)


def shards(orbitals, potential_boxes, corners, signs, counts):
    frag_dev = orbitals.shape[0]
    last_slot = frag_dev - 1
    last_count = counts[last_slot]
    filtered_list = []
    density_list = []
    for fragment in range(frag_dev):
        live_count = counts[fragment] if fragment < last_slot else last_count
        result, box_density = filter_fragment(
            orbitals[fragment], potential_boxes[fragment], live_count
        )
        filtered_list.append(result)
        density_list.append(box_density)
    filtered = jnp.stack(filtered_list)
    signed = jnp.stack(density_list) * signs.astype(jnp.float32)[:, None, None]
    paired = signed[0::2] + signed[1::2]
    pair_count = frag_dev // 2
    row_start = lax.axis_index("row") * CX
    col_start = lax.axis_index("col") * CY
    offsets = jnp.stack(
        [corners[0::2, 0] - row_start, corners[0::2, 1] - col_start, corners[0::2, 2]], axis=1
    )
    reach_x = (CX + B - 2) // CX + 1
    reach_y = (CY + B - 2) // CY + 1
    slab = jnp.zeros((reach_y * CY, reach_x * CX, NZ + B), jnp.float32)
    slab = place_all(slab, paired.reshape(pair_count, B, B, B), offsets, 0)
    slab = wrap_depth(slab)
    band = slab[:CY]
    for step in range(1, reach_y):
        band = band + passed_along(slab[step * CY : (step + 1) * CY], "col", step)
    density_yx = band[:, :CX]
    for step in range(1, reach_x):
        density_yx = density_yx + passed_along(band[:, step * CX : (step + 1) * CX], "row", step)
    density = jnp.transpose(density_yx, (1, 0, 2))
    grid_rows = CX * lax.axis_size("row")
    grid_cols = CY * lax.axis_size("col")
    cos_z, sin_z = tables(NZ)
    rho_real = jnp.einsum("yxz,zk->xky", density_yx, cos_z, precision=HIGHEST)
    rho_imag = -jnp.einsum("yxz,zk->xky", density_yx, sin_z, precision=HIGHEST)
    spectrum = lax.all_to_all(
        jnp.stack([rho_real, rho_imag]), "col", split_axis=2, concat_axis=3, tiled=True
    )
    cos_y, sin_y = tables(grid_cols)
    spec_real, spec_imag = along_last(spectrum[0], spectrum[1], cos_y, sin_y, -1.0)
    spectrum = lax.all_to_all(
        jnp.stack([spec_real, spec_imag]), "row", split_axis=2, concat_axis=1, tiled=True
    )
    cos_x, sin_x = tables(grid_rows)
    spec_real, spec_imag = along_first(spectrum[0], spectrum[1], cos_x, sin_x, -1.0)
    depth = NZ // lax.axis_size("col")
    thin_depth = depth // lax.axis_size("row")
    z_index = (
        lax.axis_index("col") * depth
        + lax.axis_index("row") * thin_depth
        + lax.iota(jnp.int32, thin_depth)
    )
    k_square = (
        wave_square(grid_rows, lax.iota(jnp.int32, grid_rows))[:, None, None]
        + wave_square(grid_cols, lax.iota(jnp.int32, grid_cols))[None, None, :]
        + wave_square(NZ, z_index)[None, :, None]
    )
    factor = jnp.where(k_square > 0, SCREEN / (k_square + SCREEN), 0.0)
    spec_real, spec_imag = along_first(spec_real * factor, spec_imag * factor, cos_x, sin_x, 1.0)
    spectrum = lax.all_to_all(
        jnp.stack([spec_real, spec_imag]), "row", split_axis=1, concat_axis=2, tiled=True
    )
    spec_real, spec_imag = along_last(spectrum[0], spectrum[1], cos_y, sin_y, 1.0)
    spectrum = lax.all_to_all(
        jnp.stack([spec_real, spec_imag]), "col", split_axis=3, concat_axis=2, tiled=True
    )
    hartree = jnp.einsum("xky,kz->xyz", spectrum[0], cos_z, precision=HIGHEST) - jnp.einsum(
        "xky,kz->xyz", spectrum[1], sin_z, precision=HIGHEST
    )
    hartree = hartree / float(grid_rows * grid_cols * NZ)
    return (filtered, density, hartree)


def solution(mesh):
    return jax.shard_map(
        shards,
        mesh=mesh,
        in_specs=(
            P(("row", "col"), None, None, None),
            P(("row", "col"), None, None),
            P(("row", "col"), None),
            P(("row", "col")),
            P(("row", "col")),
        ),
        out_specs=(
            P(("row", "col"), None, None, None),
            P("row", "col", None),
            P("row", "col", None),
        ),
        check_vma=False,
    )
```

profile of v0, /device:TPU:0, one launch (start us, length us, event | category | flops | bytes accessed | tf_op | source)
XLA Modules:
  0.0 490.9 jit_solution(2470559800561057647)
XLA Ops:
  8.0 11.7 %while.32 = (s32[]{:T(128)}, bf16[8,48,2304]{2,1,0:T(8,128)(2,1)}, f32[48,2304]{1,0:T(8,128)S(1)}, s32[]{:T(128)}, f32[48,2304]{1,0:T(8,128)S(1)}, /*index=5*/bf...) while((s32[]{:T(128)}, bf16[8,48,2304]{2,1,0:T(8,128)(2,1)}, ...), condition=%wide.region_5.6_spmd, body=%wide.region_3.5_spmd.sunk | while | flops 13174278 | bytes 60521680 | solution.py:67
  21.1 9.1 %while.31 = (s32[]{:T(128)}, bf16[8,48,2304]{2,1,0:T(8,128)(2,1)}, f32[48,2304]{1,0:T(8,128)S(1)}, s32[]{:T(128)}, f32[48,2304]{1,0:T(8,128)S(1)}, /*index=5*/bf...) while((s32[]{:T(128)}, bf16[8,48,2304]{2,1,0:T(8,128)(2,1)}, ...), condition=%wide.region_2.3_spmd, body=%wide.region_0.2_spmd.sunk | while | flops 13174278 | bytes 60521680 | solution.py:67
  35.0 4.2 broadcast_in_dim.61
  39.1 28.9 %dynamic_update_slice.18 = f32[56,64,560]{2,0,1:T(8,128)} dynamic-update-slice(f32[56,64,560]{2,0,1:T(8,128)} %broadcast_in_dim.61, f32[48,48,48]{2,0,1:T(8,128)S(1)} %bitcast.206, s32[]{:T(128)S(6)} %select_n.364, s32[]{:T(128)S(6)} %select_n.365, s32[]{:T(128)S(6)} %select_n.366) | dynamic-update-slice | bytes 884740 | tf_op jit(solution)/shard_map/dynamic_update_slice | solution.py:72
  68.1 6.9 %slice.757 = f32[56,64,512]{2,0,1:T(8,128)} slice(f32[56,64,560]{2,0,1:T(8,128)} %dynamic_update_slice.18), slice={[0:56], [0:64], [0:512]} | slice | bytes 14680064 | tf_op jit(solution)/shard_map/slice | solution.py:77
  77.2 10.4 %scatter-add.4 = f32[56,64,512]{2,0,1:T(8,128)} dynamic-update-slice(f32[56,64,512]{2,0,1:T(8,128)} %slice.757, f32[56,64,48]{2,0,1:T(8,128)S(1)} %slice_add_fusion, s32[]{:T(128)} %constant.366.clone.1, s32[]{:T(128)} %constant.366.clone.1, s32[]{:T(128)} %constant.366.clone.1) | dynamic-update-slice | bytes 1376260 | tf_op jit(solution)/shard_map/scatter-add | solution.py:78
  91.1 5.8 %collective-permute-start.5 = (f32[8,64,512]{2,0,1:T(8,128)S(1)}, f32[8,64,512]{2,0,1:T(8,128)S(1)}, u32[]{:S(2)}, u32[]{:S(2)}) collective-permute-start(f32[8,64,512]{2,0,1:T(8,128)S(1)} %get-tuple-element.356), channel_id=1, source_target_pairs={{0,6},{1,7},{2,8},{3,9},{4,10},{5,11},{6,12},{7,13},{8,14},{9,15},... | collective-permute-start | bytes 3145736 | tf_op jit(solution)/shard_map/ppermute | solution.py:23
  97.0 59.6 %collective-permute-start.4 = (f32[8,64,512]{2,0,1:T(8,128)S(1)}, f32[8,64,512]{2,0,1:T(8,128)S(1)}, u32[]{:S(2)}, u32[]{:S(2)}) collective-permute-start(f32[8,64,512]{2,0,1:T(8,128)S(1)} %get-tuple-element.357), channel_id=1, source_target_pairs={{0,5},{1,6},{2,7},{3,8},{4,9},{5,10},{6,11},{7,12},{8,13},{9,14},{... | collective-permute-start | bytes 3145736 | tf_op jit(solution)/shard_map/ppermute | solution.py:23
  156.6 56.5 %collective-permute-start.2 = (f32[8,64,512]{2,0,1:T(8,128)S(1)}, f32[8,64,512]{2,0,1:T(8,128)S(1)}, u32[]{:S(2)}, u32[]{:S(2)}) collective-permute-start(f32[8,64,512]{2,0,1:T(8,128)S(1)} %get-tuple-element.359), channel_id=1, source_target_pairs={{0,3},{1,4},{2,5},{3,6},{4,7},{5,8},{6,9},{7,10},{8,11},{9,12},{10... | collective-permute-start | bytes 3145736 | tf_op jit(solution)/shard_map/ppermute | solution.py:23
  213.9 18.1 %collective-permute-start = (f32[8,64,512]{2,0,1:T(8,128)S(1)}, f32[8,64,512]{2,0,1:T(8,128)S(1)}, u32[]{:S(2)}, u32[]{:S(2)}) collective-permute-start(f32[8,64,512]{2,0,1:T(8,128)S(1)} %get-tuple-element.355), channel_id=1, source_target_pairs={{0,1},{1,2},{2,3},{3,4},{4,5},{5,6},{6,7},{7,8},{8,9},{9,10},{10,1... | collective-permute-start | bytes 3145736 | tf_op jit(solution)/shard_map/ppermute | solution.py:23
  232.0 37.8 %collective-permute-done.3 = f32[8,64,512]{2,0,1:T(8,128)S(1)} collective-permute-done((f32[8,64,512]{2,0,1:T(8,128)S(1)}, f32[8,64,512]{2,0,1:T(8,128)S(1)}, u32[]{:S(2)}, u32[]{:S(2)}) %collective-permute-start.3) | collective-permute-done | bytes 1048608 | tf_op jit(solution)/shard_map/ppermute | solution.py:23
  272.0 36.6 %collective-permute-start.8 = (f32[8,16,512]{2,0,1:T(8,128)S(1)}, f32[8,16,512]{2,0,1:T(8,128)S(1)}, u32[]{:S(2)}, u32[]{:S(2)}) collective-permute-start(f32[8,16,512]{2,0,1:T(8,128)S(1)} %get-tuple-element.368), channel_id=1, source_target_pairs={{0,96},{32,0},{64,32},{96,64},{1,97},{33,1},{65,33},{97,65},{2,98}... | collective-permute-start | bytes 786440 | tf_op jit(solution)/shard_map/ppermute | solution.py:23
  314.4 8.0 %collective-permute-done.7 = f32[8,16,512]{2,0,1:T(8,128)S(1)} collective-permute-done((f32[8,16,512]{2,0,1:T(8,128)S(1)}, f32[8,16,512]{2,0,1:T(8,128)S(1)}, u32[]{:S(2)}, u32[]{:S(2)}) %collective-permute-start.7) | collective-permute-done | bytes 262176 | tf_op jit(solution)/shard_map/ppermute | solution.py:23
  322.6 5.1 %fusion.180 = f32[1,16,512,8]{2,1,3,0:T(8,128)S(1)} fusion(f32[8,16,512]{2,0,1:T(8,128)S(1)} %fusion.210), kind=kOutput, calls=%fused_computation.203 | convolution fusion | flops 406388736 | bytes 524288 | tf_op jit(solution)/shard_map/yxz,zk->xky/dot_general | solution.py:153
  327.7 5.0 %convolution_bitcast_fusion = f32[1,16,512,8]{2,1,3,0:T(8,128)S(1)} fusion(f32[8,16,512]{2,0,1:T(8,128)S(1)} %fusion.210), kind=kOutput, calls=%fused_computation.204 | convolution fusion | flops 406323200 | bytes 524288 | tf_op jit(solution)/shard_map/yxz,zk->xky/dot_general | solution.py:152
  336.4 4.2 reshape.129
  340.6 15.8 %all-to-all-start = ((f32[32,1,4096]{2,1,0:T(1,128)}), f32[32,1,4096]{2,1,0:T(1,128)S(1)}, u32[]{:S(2)}, u32[]{:S(2)}) async-start(f32[32,1,4096]{2,1,0:T(1,128)} %reshape.129), calls=%async_computation | async-start | bytes 1048576 | tf_op jit(solution)/shard_map/all_to_all | solution.py:154
  356.4 12.6 %all-to-all-done = f32[32,1,4096]{2,1,0:T(1,128)S(1)} async-done(((f32[32,1,4096]{2,1,0:T(1,128)}), f32[32,1,4096]{2,1,0:T(1,128)S(1)}, u32[]{:S(2)}, u32[]{:S(2)}) %all-to-all-start) | async-done | bytes 524320 | tf_op jit(solution)/shard_map/all_to_all | solution.py:154
  374.2 6.9 %copy.56 = f32[2,16,32,16,8]{3,2,4,1,0:T(8,128)} copy(f32[2,16,32,16,8]{1,4,0,3,2:T(8,128)} %bitcast.202) | data formatting | bytes 1048576 | tf_op jit(solution)/shard_map/all_to_all | solution.py:154
  383.9 4.6 fusion.142
  388.5 4.6 fusion.169
  393.1 4.6 fusion.166
  397.7 4.7 fusion.157
  407.1 8.7 %all-to-all-done.1 = f32[2,16,16,256]{3,1,0,2:T(8,128)S(1)} async-done(((f32[2,16,16,256]{3,1,0,2:T(8,128)}), f32[2,16,16,256]{3,1,0,2:T(8,128)S(1)}, u32[]{:S(2)}, u32[]{:S(2)}) %all-to-all-start.1) | async-done | bytes 524320 | tf_op jit(solution)/shard_map/all_to_all | solution.py:159
  420.4 11.4 %all_to_all.60 = f32[2,64,4,256]{3,2,0,1:T(4,128)S(1)} all-to-all(f32[2,64,4,256]{3,2,0,1:T(4,128)S(1)} %copy.46), channel_id=1, replica_groups=mesh['row'=4,'col'=32] {'row'}, dimensions={1} | all-to-all | bytes 1048576 | tf_op jit(solution)/shard_map/all_to_all | solution.py:178
  437.7 4.4 copy.48
  442.1 4.4 reshape.131
  446.4 4.9 all-to-all-start.3
  453.4 10.9 %all-to-all-done.3 = f32[32,1,4096]{2,1,0:T(1,128)} async-done(((f32[32,1,4096]{2,1,0:T(1,128)}), f32[32,1,4096]{2,1,0:T(1,128)}, u32[]{:S(2)}, u32[]{:S(2)}) %all-to-all-start.3) | async-done | bytes 524320 | tf_op jit(solution)/shard_map/all_to_all | solution.py:182
  470.0 4.6 copy.92
  478.3 4.8 fusion.192
  485.1 5.4 %fusion.181 = f32[16,8,512]{2,1,0:T(8,128)} fusion(f32[16,8,512]{2,1,0:T(8,128)S(1)} %fusion.192, f32[16,512,8]{1,2,0:T(8,128)S(1)} %squeeze.74), kind=kOutput, calls=%fused_computation.206 | convolution fusion | flops 406454272 | bytes 786432 | tf_op jit(solution)/shard_map/xky,kz->xyz/dot_general | solution.py:185
  (140 shorter events, 81.6 us)
Async XLA Ops:
  21.1 9.1 %copy-start.5 = (s32[2]{0:T(128)S(1)}, s32[2]{0:T(128)}, u32[]{:S(2)}) copy-start(s32[2]{0:T(128)} %param.14) | copy-start | bytes 28
  30.2 0.9 copy-start.4
  91.1 122.8 %collective-permute-start.5 = (f32[8,64,512]{2,0,1:T(8,128)S(1)}, f32[8,64,512]{2,0,1:T(8,128)S(1)}, u32[]{:S(2)}, u32[]{:S(2)}) collective-permute-start(f32[8,64,512]{2,0,1:T(8,128)S(1)} %get-tuple-element.356), channel_id=1, source_target_pairs={{0,6},{1,7},{2,8},{3,9},{4,10},{5,11},{6,12},{7,13},{8,14},{9,15},... | collective-permute-start | bytes 3145736 | tf_op jit(solution)/shard_map/ppermute | solution.py:23
  97.0 135.0 %collective-permute-start.4 = (f32[8,64,512]{2,0,1:T(8,128)S(1)}, f32[8,64,512]{2,0,1:T(8,128)S(1)}, u32[]{:S(2)}, u32[]{:S(2)}) collective-permute-start(f32[8,64,512]{2,0,1:T(8,128)S(1)} %get-tuple-element.357), channel_id=1, source_target_pairs={{0,5},{1,6},{2,7},{3,8},{4,9},{5,10},{6,11},{7,12},{8,13},{9,14},{... | collective-permute-start | bytes 3145736 | tf_op jit(solution)/shard_map/ppermute | solution.py:23
  156.6 113.2 %collective-permute-start.3 = (f32[8,64,512]{2,0,1:T(8,128)S(1)}, f32[8,64,512]{2,0,1:T(8,128)S(1)}, u32[]{:S(2)}, u32[]{:S(2)}) collective-permute-start(f32[8,64,512]{2,0,1:T(8,128)S(1)} %get-tuple-element.358), channel_id=1, source_target_pairs={{0,4},{1,5},{2,6},{3,7},{4,8},{5,9},{6,10},{7,11},{8,12},{9,13},{1... | collective-permute-start | bytes 3145736 | tf_op jit(solution)/shard_map/ppermute | solution.py:23
  156.6 113.2 %collective-permute-start.2 = (f32[8,64,512]{2,0,1:T(8,128)S(1)}, f32[8,64,512]{2,0,1:T(8,128)S(1)}, u32[]{:S(2)}, u32[]{:S(2)}) collective-permute-start(f32[8,64,512]{2,0,1:T(8,128)S(1)} %get-tuple-element.359), channel_id=1, source_target_pairs={{0,3},{1,4},{2,5},{3,6},{4,7},{5,8},{6,9},{7,10},{8,11},{9,12},{10... | collective-permute-start | bytes 3145736 | tf_op jit(solution)/shard_map/ppermute | solution.py:23
  213.1 56.7 %collective-permute-start.1 = (f32[8,64,512]{2,0,1:T(8,128)S(1)}, f32[8,64,512]{2,0,1:T(8,128)S(1)}, u32[]{:S(2)}, u32[]{:S(2)}) collective-permute-start(f32[8,64,512]{2,0,1:T(8,128)S(1)} %get-tuple-element.360), channel_id=1, source_target_pairs={{0,2},{1,3},{2,4},{3,5},{4,6},{5,7},{6,8},{7,9},{8,10},{9,11},{10,... | collective-permute-start | bytes 3145736 | tf_op jit(solution)/shard_map/ppermute | solution.py:23
  213.9 55.9 %collective-permute-start = (f32[8,64,512]{2,0,1:T(8,128)S(1)}, f32[8,64,512]{2,0,1:T(8,128)S(1)}, u32[]{:S(2)}, u32[]{:S(2)}) collective-permute-start(f32[8,64,512]{2,0,1:T(8,128)S(1)} %get-tuple-element.355), channel_id=1, source_target_pairs={{0,1},{1,2},{2,3},{3,4},{4,5},{5,6},{6,7},{7,8},{8,9},{9,10},{10,1... | collective-permute-start | bytes 3145736 | tf_op jit(solution)/shard_map/ppermute | solution.py:23
  272.0 42.5 %collective-permute-start.8 = (f32[8,16,512]{2,0,1:T(8,128)S(1)}, f32[8,16,512]{2,0,1:T(8,128)S(1)}, u32[]{:S(2)}, u32[]{:S(2)}) collective-permute-start(f32[8,16,512]{2,0,1:T(8,128)S(1)} %get-tuple-element.368), channel_id=1, source_target_pairs={{0,96},{32,0},{64,32},{96,64},{1,97},{33,1},{65,33},{97,65},{2,98}... | collective-permute-start | bytes 786440 | tf_op jit(solution)/shard_map/ppermute | solution.py:23
  308.6 13.9 %collective-permute-start.7 = (f32[8,16,512]{2,0,1:T(8,128)S(1)}, f32[8,16,512]{2,0,1:T(8,128)S(1)}, u32[]{:S(2)}, u32[]{:S(2)}) collective-permute-start(f32[8,16,512]{2,0,1:T(8,128)S(1)} %get-tuple-element.369), channel_id=1, source_target_pairs={{0,64},{32,96},{64,0},{96,32},{1,65},{33,97},{65,1},{97,33},{2,66}... | collective-permute-start | bytes 786440 | tf_op jit(solution)/shard_map/ppermute | solution.py:23
  309.9 12.5 %collective-permute-start.6 = (f32[8,16,512]{2,0,1:T(8,128)S(1)}, f32[8,16,512]{2,0,1:T(8,128)S(1)}, u32[]{:S(2)}, u32[]{:S(2)}) collective-permute-start(f32[8,16,512]{2,0,1:T(8,128)S(1)} %get-tuple-element.367), channel_id=1, source_target_pairs={{0,32},{32,64},{64,96},{96,0},{1,33},{33,65},{65,97},{97,1},{2,34}... | collective-permute-start | bytes 786440 | tf_op jit(solution)/shard_map/ppermute | solution.py:23
  322.5 5.1 %copy-start.3 = (f32[8,16,512]{2,0,1:T(8,128)}, f32[8,16,512]{2,0,1:T(8,128)S(1)}, u32[]{:S(2)}) copy-start(f32[8,16,512]{2,0,1:T(8,128)S(1)} %fusion.210) | copy-start | bytes 786436
  340.6 28.4 %all-to-all-start = ((f32[32,1,4096]{2,1,0:T(1,128)}), f32[32,1,4096]{2,1,0:T(1,128)S(1)}, u32[]{:S(2)}, u32[]{:S(2)}) async-start(f32[32,1,4096]{2,1,0:T(1,128)} %reshape.129), calls=%async_computation | async-start | bytes 1048576 | tf_op jit(solution)/shard_map/all_to_all | solution.py:154
  403.6 12.3 %all-to-all-start.1 = ((f32[2,16,16,256]{3,1,0,2:T(8,128)}), f32[2,16,16,256]{3,1,0,2:T(8,128)S(1)}, u32[]{:S(2)}, u32[]{:S(2)}) async-start(f32[2,16,16,256]{3,1,0,2:T(8,128)} %copy.44), calls=%async_computation.1 | async-start | bytes 1048576 | tf_op jit(solution)/shard_map/all_to_all | solution.py:159
  442.1 9.2 %copy-start.1 = (bf16[8,48,2304]{2,1,0:T(8,128)(2,1)S(1)}, bf16[8,48,2304]{2,1,0:T(8,128)(2,1)}, u32[]{:S(2)}) copy-start(bf16[8,48,2304]{2,1,0:T(8,128)(2,1)} %get-tuple-element.239) | copy-start | bytes 5308420
  442.1 9.2 %copy-start.2 = (bf16[8,48,2304]{2,1,0:T(8,128)(2,1)S(1)}, bf16[8,48,2304]{2,1,0:T(8,128)(2,1)}, u32[]{:S(2)}) copy-start(bf16[8,48,2304]{2,1,0:T(8,128)(2,1)} %get-tuple-element.240) | copy-start | bytes 5308420
  446.4 17.9 %all-to-all-start.3 = ((f32[32,1,4096]{2,1,0:T(1,128)}), f32[32,1,4096]{2,1,0:T(1,128)}, u32[]{:S(2)}, u32[]{:S(2)}) async-start(f32[32,1,4096]{2,1,0:T(1,128)} %reshape.131), calls=%async_computation.3 | async-start | bytes 1048576 | tf_op jit(solution)/shard_map/all_to_all | solution.py:182
  478.3 4.9 copy-start
where the time goes:
time: 501 us; the launch traced here: 491 us
  starting transfers between devices  203 us (41%)
  local copies, waits for them, and re-layouts  114 us (23%)
  waiting for transfers between devices  82.1 us (16%)
  matrix products  48.3 us (10%)
  other arithmetic  23 us (5%)
  blocking collectives  11.4 us (2%)
    ppermute x9, starting transfers between devices, passed_along(): lax.ppermute(value, axis, [(i, (i + by) % peers) for i in range(peers)])  179 us
    ppermute x9, waiting for transfers between devices, passed_along(): lax.ppermute(value, axis, [(i, (i + by) % peers) for i in range(peers)])  50 us
    dynamic_update_slice x1, local copies, waits for them, and re-layouts, place_all(): lax.dynamic_update_slice(slab, jnp.transpose(cubes[0], (1, 0, 2)), start)  28.9 us
    all_to_all x1, starting transfers between devices, shards(): lax.all_to_all(jnp.stack([rho_real, rho_imag]), 'col', split_axis=2, conc...  15.8 us
    unnamed x16, local copies, waits for them, and re-layouts  14.2 us
    all_to_all x1, waiting for transfers between devices, shards(): lax.all_to_all(jnp.stack([rho_real, rho_imag]), 'col', split_axis=2, conc...  12.6 us
    all_to_all x1, blocking collectives, shards(): lax.all_to_all(jnp.stack([spec_real, spec_imag]), 'row', split_axis=1, co...  11.4 us
    all_to_all x1, waiting for transfers between devices, shards(): lax.all_to_all(jnp.stack([spec_real, spec_imag]), 'col', split_axis=3, co...  10.9 us
  transfers between devices with their start and end apart: 12, of which 6 were waited for; matrix products, arithmetic and copies ran while one was open for 0% of the time, Pallas kernels for 0%

commit v1 on v0

v1 whole, which is shorter than its diff:
```python
import math

import jax
import jax.numpy as jnp
import numpy as np
from jax import lax
from jax.experimental import pallas as pl
from jax.experimental.pallas import tpu as pltpu
from jax.sharding import PartitionSpec as P

B = 48
YZ = B * B
TILES = YZ // 128
ORB = 8
LANES = 128
NX, NY, NZ = 64, 256, 512
CX, CY = 16, 8
SCREEN = 0.0025
BOTH = ("row", "col")
F32 = jnp.float32
BF16 = jnp.bfloat16

ROOTS = [7.5 * math.cos(math.pi * k / 12) for k in (1, 11, 5, 9, 3, 7)]
KAPPA = 32.0 / 7.5**6
PIECE = 56
NT = (((1,), (1,)), ((), ()))
NN = (((1,), (0,)), ((), ()))


def dot(a, b, dims=NN):
    return lax.dot_general(a, b, dims, preferred_element_type=F32)


def split(v):
    high = v.astype(BF16)
    return high, (v - high.astype(F32)).astype(BF16)


def dot_left(tab_h, tab_l, v, dims=NN):
    h, l = split(v)
    return dot(tab_h, h, dims) + (dot(tab_h, l, dims) + dot(tab_l, h, dims))


def dot_right(v, tab_h, tab_l, dims=NN):
    h, l = split(v)
    return dot(h, tab_h, dims) + (dot(l, tab_h, dims) + dot(h, tab_l, dims))


def cheb_kernel(meta, orb, pot, eye, sel, filt, send, buf_a, buf_b, diag, stage, box):
    lane = lax.broadcasted_iota(jnp.int32, (8, LANES), 1)
    sub = lax.broadcasted_iota(jnp.int32, (8, LANES), 0)
    first_x = lane % 8 == 0
    last_x = lane % 8 == 7
    zero = jnp.zeros((8, LANES), F32)
    for buf in (buf_a, buf_b):
        for xi in range(6):
            for k in range(6):
                buf[xi, 8 * k : 8 * k + 8, :] = zero
                buf[xi, 48 + YZ + 8 * k : 56 + YZ + 8 * k, :] = zero

    @pl.loop(0, TILES)
    def _(t):
        cols = pl.ds(pl.multiple_of(t * LANES, LANES), LANES)
        for f in range(2):
            stage[f * B : (f + 1) * B, :] = 4.5 - 2.0 * pot[f, :, cols]
        for xi in range(6):
            halves = [stage[pl.ds(f * B + xi, 8, stride=6), :] for f in range(2)]
            block = jnp.concatenate([halves[0]] * 8 + [halves[1]] * 8, 0)
            diag[xi, pl.ds(pl.multiple_of(t * LANES, LANES), LANES), :] = block.T

    @pl.loop(0, TILES)
    def _(t):
        cols = pl.ds(pl.multiple_of(t * LANES, LANES), LANES)
        for fo in range(16):
            stage[fo * B : (fo + 1) * B, :] = orb[fo, :, cols].astype(F32)
        for xi in range(6):
            block = jnp.concatenate(
                [stage[pl.ds(fo * B + xi, 8, stride=6), :] for fo in range(16)], 0
            )
            out = dot(eye[...], block.astype(BF16), NT)
            buf_a[xi, pl.ds(pl.multiple_of(48 + t * LANES, 16), LANES), :] = out

    def apply(src, dst, root, acc):
        def row(y, acc):
            base = pl.multiple_of(48 + 48 * y, 16)
            dbase = pl.multiple_of(48 * y, 16)
            for zt in range(6):
                r = base + 8 * zt
                mid = [src[xi, pl.ds(r, 8), :] for xi in range(6)]
                low = jnp.where(first_x, 0.0, pltpu.roll(mid[5], 1, 1))
                high = jnp.where(last_x, 0.0, pltpu.roll(mid[0], LANES - 1, 1))
                for xi in range(6):
                    below = src[xi, pl.ds(r - 1, 8), :]
                    above = src[xi, pl.ds(r + 1, 8), :]
                    if zt == 0:
                        below = jnp.where(sub == 0, 0.0, below)
                    if zt == 5:
                        above = jnp.where(sub == 7, 0.0, above)
                    beside = (src[xi, pl.ds(r - 48, 8), :] + src[xi, pl.ds(r + 48, 8), :]) + (
                        below + above
                    )
                    left = mid[xi - 1] if xi > 0 else low
                    right = mid[xi + 1] if xi < 5 else high
                    beside = beside + (left + right)
                    d = diag[xi, pl.ds(dbase + 8 * zt, 8), :]
                    out = (d - root) * mid[xi] + beside
                    dst[xi, pl.ds(r, 8), :] = out
                    if acc is not None:
                        acc = acc + out * out
            return acc

        if acc is None:

            @pl.loop(0, B)
            def _(y):
                row(y, None)

            return None
        return lax.fori_loop(0, B, row, acc)

    apply(buf_a, buf_b, ROOTS[0], None)
    apply(buf_b, buf_a, ROOTS[1], None)
    apply(buf_a, buf_b, ROOTS[2], None)
    apply(buf_b, buf_a, ROOTS[3], None)
    apply(buf_a, buf_b, ROOTS[4], None)
    total = apply(buf_b, buf_a, ROOTS[5], zero)

    total = jnp.broadcast_to(jnp.sum(total, axis=0, keepdims=True), (8, LANES))
    for step in (1, 2, 4):
        other = jnp.where(
            lane & step == 0,
            pltpu.roll(total, LANES - step, 1),
            pltpu.roll(total, step, 1),
        )
        total = total + other
    scale = KAPPA * lax.rsqrt(total * (KAPPA * KAPPA / B**3) + 1e-6)
    second = lane >= 64
    count = jnp.where(second, meta[4], meta[3])
    sign = jnp.where(second, meta[6], meta[5]).astype(F32)
    scale = jnp.where((lane // 8) % 8 < count, scale, 0.0)
    weight = (scale * scale * sign)[:1, :]
    scale = scale[:1, :]

    @pl.loop(0, 26)
    def _(t):
        for k in range(10):
            box[t, 8 * k : 8 * k + 8, :] = zero

    @pl.loop(0, TILES)
    def _(t):
        cols = pl.ds(pl.multiple_of(t * LANES, LANES), LANES)
        for xi in range(6):
            field = buf_a[xi, pl.ds(pl.multiple_of(48 + t * LANES, 16), LANES), :]
            out = dot(eye[...], (field * scale).astype(BF16), NT)
            for fo in range(16):
                stage[pl.ds(fo * B + xi, 8, stride=6), :] = out[8 * fo : 8 * fo + 8, :]
            dh, dl = split(field * field * weight)
            dens = dot(sel[...], dh, NT) + dot(sel[...], dl, NT)
            box[t + 4, pl.ds(16 + xi, 8, stride=6), :] = dens
        for fo in range(16):
            filt[fo, :, cols] = stage[fo * B : (fo + 1) * B, :].astype(BF16)

    shift_x = meta[0]
    lanes_y = meta[1] * B
    whole = lanes_y // LANES
    rest = lanes_y % LANES
    keep = lane < LANES - rest
    zvec = jnp.full((8, LANES), meta[2], jnp.int32).astype(F32)
    for j in range(7):
        for i in range(4):
            send[j, i, 48:56, :] = zvec

    @pl.loop(0, 7)
    def _(j):
        for tt in range(3):
            t0 = 3 * j + tt - whole + 4
            for k in range(8):
                rows = pl.ds(16 + 8 * k - shift_x, 8)
                merged = jnp.where(keep, box[t0, rows, :], box[t0 - 1, rows, :])
                r0 = tt * 16 + (k % 2) * 8
                send[j, (k // 2 + meta[7]) % 4, r0 : r0 + 8, :] = pltpu.roll(merged, rest, 1)


def filter_and_box(meta, orbitals, potential, eye, sel):
    vm = pl.BlockSpec(memory_space=pltpu.VMEM)
    return pl.pallas_call(
        cheb_kernel,
        out_shape=(
            jax.ShapeDtypeStruct((16, B, YZ), BF16),
            jax.ShapeDtypeStruct((7, 4, PIECE, LANES), F32),
        ),
        in_specs=[pl.BlockSpec(memory_space=pltpu.SMEM), vm, vm, vm, vm],
        out_specs=(vm, vm),
        scratch_shapes=[
            pltpu.VMEM((6, YZ + 96, LANES), F32),
            pltpu.VMEM((6, YZ + 96, LANES), F32),
            pltpu.VMEM((6, YZ, LANES), F32),
            pltpu.VMEM((16 * B, LANES), F32),
            pltpu.VMEM((26, 80, LANES), F32),
        ],
        compiler_params=pltpu.CompilerParams(vmem_limit_bytes=60 * 1024 * 1024),
        name="cheb",
    )(meta, orbitals, potential, eye, sel)


def slot_of(lane):
    return (lane // 16) % 4


def patch_kernel(pieces, tab_h, tab_l, dens, out, grid):
    lane = lax.broadcasted_iota(jnp.int32, (8, LANES), 1)
    zero = jnp.zeros((8, LANES), F32)
    for a in range(4):
        for k in range(16):
            grid[a, 8 * k : 8 * k + 8, :] = zero
    for p in range(28):
        z0 = jnp.max(pieces[p, 48:56, :]).astype(jnp.int32)
        for y in range(8):
            tile, off = (B * y) // LANES, (B * y) % LANES
            for k in range(2):
                v = pieces[p, tile * 16 + 8 * k : tile * 16 + 8 * k + 8, :]
                if off + B > LANES:
                    w = pieces[p, tile * 16 + 16 + 8 * k : tile * 16 + 24 + 8 * k, :]
                    v = jnp.where(lane >= off, v, w)
                    window = (lane >= off) | (lane < off + B - LANES)
                else:
                    window = (lane >= off) & (lane < off + B)
                v = jnp.where(window, v, 0.0)
                amount = (z0 - off + LANES) % LANES
                v = pltpu.roll(v, amount, 1)
                a = z0 // LANES
                start = z0 % LANES
                rows = pl.ds(y * 16 + 8 * k, 8)
                grid[a, rows, :] = grid[a, rows, :] + jnp.where(lane >= start, v, 0.0)
                nxt = (a + 1) % 4
                grid[nxt, rows, :] = grid[nxt, rows, :] + jnp.where(lane >= start, 0.0, v)
    for x in range(16):
        for a in range(4):
            dens[x, :, a * LANES : (a + 1) * LANES] = grid[a, pl.ds(x, 8, stride=16), :]
    rho = jnp.concatenate([grid[a] for a in range(4)], 1)
    spec = dot_left(tab_h[...], tab_l[...], rho, NT)
    slot = slot_of(lax.broadcasted_iota(jnp.int32, (LANES, LANES), 1))
    for q in range(4):
        final = spec[q * LANES : (q + 1) * LANES, :]
        for m in range(4):
            if m != q:
                part = pltpu.roll(spec[m * LANES : (m + 1) * LANES, :], (16 * (m - q)) % LANES, 1)
                final = jnp.where(slot == m, part, final)
        out[pl.ds(q, LANES, stride=4), :] = final


def patch(pieces, tab_h, tab_l):
    vm = pl.BlockSpec(memory_space=pltpu.VMEM)
    return pl.pallas_call(
        patch_kernel,
        out_shape=(
            jax.ShapeDtypeStruct((CX, CY, NZ), F32),
            jax.ShapeDtypeStruct((512, LANES), F32),
        ),
        in_specs=[vm] * 3,
        out_specs=(vm, vm),
        scratch_shapes=[pltpu.VMEM((4, LANES, LANES), F32)],
        name="patch",
    )(pieces, tab_h, tab_l)


def middle_kernel(data, kxz, ky, ry, ryt, bx, bxt, out):
    slab = jnp.concatenate([data[r * LANES : (r + 1) * LANES, :] for r in range(4)], 1)
    both = dot_left(ry[0], ry[1], slab)
    wide = lax.broadcasted_iota(jnp.int32, (1, 512), 1)
    upper = wide % LANES >= 64
    mixed = jnp.where(upper, both[256:], both[:256])
    spec = dot_right(mixed, bx[0], bx[1])
    k_square = (kxz[0:1, :] + ky[...]) + kxz[1:2, :]
    factor = jnp.where(k_square > 0, SCREEN / (k_square + SCREEN), 0.0)
    back = dot_right(spec * factor, bxt[0], bxt[1])
    both = dot_left(ryt[0], ryt[1], back)
    mixed = jnp.where(upper, both[LANES:], both[:LANES])
    for r in range(4):
        out[r * LANES : (r + 1) * LANES, :] = mixed[:, r * LANES : (r + 1) * LANES]


def middle(data, kxz, ky, ry, ryt, bx, bxt):
    vm = pl.BlockSpec(memory_space=pltpu.VMEM)
    return pl.pallas_call(
        middle_kernel,
        out_shape=jax.ShapeDtypeStruct((512, LANES), F32),
        in_specs=[vm] * 7,
        out_specs=vm,
        name="middle",
    )(data, kxz, ky, ry, ryt, bx, bxt)


def final_kernel(data, tab_h, tab_l, hart, grid):
    slot = slot_of(lax.broadcasted_iota(jnp.int32, (LANES, LANES), 1))
    parts = [data[pl.ds(q, LANES, stride=4), :] for q in range(4)]
    blocks = []
    for m in range(4):
        block = parts[m]
        for q in range(4):
            if q != m:
                block = jnp.where(slot == q, pltpu.roll(parts[q], (16 * (q - m)) % LANES, 1), block)
        blocks.append(block.T)
    spec = jnp.concatenate(blocks, 1)
    field = dot_right(spec, tab_h[...], tab_l[...])
    for a in range(4):
        grid[a] = field[:, a * LANES : (a + 1) * LANES]
    for x in range(16):
        for a in range(4):
            hart[x, :, a * LANES : (a + 1) * LANES] = grid[a, pl.ds(x, 8, stride=16), :]


def final(data, tab_h, tab_l):
    vm = pl.BlockSpec(memory_space=pltpu.VMEM)
    return pl.pallas_call(
        final_kernel,
        out_shape=jax.ShapeDtypeStruct((CX, CY, NZ), F32),
        in_specs=[vm] * 3,
        out_specs=vm,
        scratch_shapes=[pltpu.VMEM((4, LANES, LANES), F32)],
        name="final",
    )(data, tab_h, tab_l)


def real_basis(n):
    index = np.arange(n)
    angle = 2 * np.pi * (np.outer(index, index) % n) / n
    basis = np.where((index <= n // 2)[:, None], np.cos(angle), np.sin(angle)) * np.sqrt(2 / n)
    basis[0] = np.sqrt(1 / n)
    basis[n // 2] = np.where(index % 2 == 0, 1, -1) * np.sqrt(1 / n)
    return basis


def halves(table):
    table = np.ascontiguousarray(table).astype(np.float32)
    high = table.astype(BF16)
    low = (table - high.astype(np.float32)).astype(BF16)
    return high, low


def wave_square(length, positions):
    signed = np.where(positions <= length // 2, positions, positions - length)
    wave = signed.astype(np.float32) * np.float32(2 * math.pi / length)
    return wave * wave


def constants():
    rz = real_basis(NZ)
    ry = real_basis(NY).reshape(NY, 32, 2, 4).transpose(2, 0, 1, 3).reshape(2 * NY, LANES)
    ryt = ry.reshape(2, NY, LANES).transpose(0, 2, 1).reshape(2 * LANES, NY)
    rx = real_basis(NX).reshape(NX, 4, 16)
    bx = np.einsum("krx,mn->rmxnk", rx, np.eye(4))
    bx = np.broadcast_to(bx[:, None], (4, 2, 4, 16, 4, NX)).reshape(512, 256)
    return dict(
        rz=halves(rz),
        ry=np.stack(halves(ry)),
        ryt=np.stack(halves(ryt)),
        bx=np.stack(halves(bx)),
        bxt=np.stack(halves(bx.T)),
        eye=np.eye(LANES).astype(BF16),
        sel=(np.arange(LANES)[None, :] % 8 == np.arange(8)[:, None]).astype(BF16),
        ky=wave_square(NY, np.arange(NY)).reshape(NY, 1),
        kx=np.tile(wave_square(NX, np.arange(NX)), 4),
        kz=wave_square(NZ, np.arange(NZ)),
    )


def passed_along(value, axis, by):
    peers = lax.axis_size(axis)
    return lax.ppermute(value, axis, [(i, (i + by) % peers) for i in range(peers)])


def shards(orbitals, potential_boxes, corners, signs, counts):
    tab = constants()
    meta = jnp.stack(
        [
            corners[0, 0] % CX,
            corners[0, 1] % CY,
            corners[0, 2],
            counts[0],
            counts[1],
            signs[0],
            signs[1],
            lax.axis_index("row").astype(jnp.int32),
        ]
    )
    filtered, send = filter_and_box(
        meta, orbitals.reshape(16, B, YZ), potential_boxes, tab["eye"], tab["sel"]
    )
    parts = [send[0]] + [passed_along(send[j], "col", j) for j in range(1, 7)]
    pieces = lax.all_to_all(
        jnp.stack(parts, axis=1), "row", split_axis=0, concat_axis=0, tiled=True
    ).reshape(28, PIECE, LANES)
    density, packed = patch(pieces, *tab["rz"])
    packed = lax.all_to_all(packed, BOTH, split_axis=0, concat_axis=0, tiled=True)
    device = lax.axis_index("row") * 32 + lax.axis_index("col")
    kz = lax.dynamic_slice(jnp.asarray(tab["kz"]).reshape(4, LANES), (0, device), (4, 1))
    kxz = jnp.stack([jnp.asarray(tab["kx"]), jnp.repeat(kz[:, 0], NX)])
    packed = middle(packed, kxz, tab["ky"], tab["ry"], tab["ryt"], tab["bx"], tab["bxt"])
    packed = lax.all_to_all(packed, BOTH, split_axis=0, concat_axis=0, tiled=True)
    hartree = final(packed, *tab["rz"])
    return (filtered.reshape(2, ORB, B, YZ), density, hartree)


def solution(mesh):
    return jax.shard_map(
        shards,
        mesh=mesh,
        in_specs=(
            P(BOTH, None, None, None),
            P(BOTH, None, None),
            P(BOTH, None),
            P(BOTH),
            P(BOTH),
        ),
        out_specs=(
            P(BOTH, None, None, None),
            P("row", "col", None),
            P("row", "col", None),
        ),
        check_vma=False,
    )
```

time: 501 us -> 146 us (0.29); the launches traced: 491 us -> 144 us
  starting transfers between devices: 203 us -> 24.2 us
  local copies, waits for them, and re-layouts: 114 us -> 7.17 us
  waiting for transfers between devices: 82.1 us -> 14.7 us
  Pallas kernels: 0 us -> 61.8 us
  matrix products: 48.3 us -> 0 us
  other arithmetic: 23 us -> 0.58 us
  blocking collectives: 11.4 us -> 31.2 us
    ppermute x9 -> x6, starting transfers between devices: 179 us -> 18 us  [passed_along(): lax.ppermute(value, axis, [(i, (i + by) % peers) for i in range(peers)])]
    pallas_call x0 -> x4, Pallas kernels: none -> 61.8 us  [the longest x1 47.5 us: filter_and_box(): pl.pallas_call(cheb_kernel, out_shape=(jax.ShapeDtypeStruct((16, B, YZ),...]
    dot_general x20 -> x0, matrix products: 48.3 us -> none  [the longest x2 6.08 us: along_last(): real_cos = jnp.einsum('abn,nk->abk', real_part, cosines, precision=HIGHEST)]
    ppermute x9 -> x6, waiting for transfers between devices: 50 us -> 5.38 us  [passed_along(): lax.ppermute(value, axis, [(i, (i + by) % peers) for i in range(peers)])]
    dynamic_update_slice x1 -> x0, local copies, waits for them, and re-layouts: 28.9 us -> none  [place_all(): lax.dynamic_update_slice(slab, jnp.transpose(cubes[0], (1, 0, 2)), start)]
    all_to_all x3 -> x1, waiting for transfers between devices: 32.1 us -> 9.29 us  [shards(): lax.all_to_all(packed, BOTH, split_axis=0, concat_axis=0, tiled=True)]
    slice x47 -> x1, local copies, waits for them, and re-layouts: 23 us -> 1.38 us  [shards(): corners[0, 2]]
    all_to_all x1 -> x2, blocking collectives: 11.4 us -> 31.2 us  [the longest x1 16.2 us: shards(): lax.all_to_all(packed, BOTH, split_axis=0, concat_axis=0, tiled=True)]
  transfers between devices with their start and end apart: 12 -> 7, of which waited for: 6 -> 3; matrix products, arithmetic and copies ran while one was open for 0% -> 2% of each run, Pallas kernels for 0% -> 0%
where the time goes in v1:
time: 146 us; the launch traced here: 144 us
  Pallas kernels  61.8 us (42%)
  blocking collectives  31.2 us (21%)
  starting transfers between devices  24.2 us (17%)
  waiting for transfers between devices  14.7 us (10%)
  local copies, waits for them, and re-layouts  7.17 us (5%)
  between operations  4.65 us (3%)
    pallas_call x1, Pallas kernels, filter_and_box(): pl.pallas_call(cheb_kernel, out_shape=(jax.ShapeDtypeStruct((16, B, YZ),...  47.5 us
    ppermute x6, starting transfers between devices, passed_along(): lax.ppermute(value, axis, [(i, (i + by) % peers) for i in range(peers)])  18 us
    all_to_all x1, blocking collectives, shards(): lax.all_to_all(packed, BOTH, split_axis=0, concat_axis=0, tiled=True)  16.2 us
    all_to_all x1, blocking collectives, shards(): lax.all_to_all(jnp.stack(parts, axis=1), 'row', split_axis=0, concat_axis...  14.9 us
    all_to_all x1, waiting for transfers between devices, shards(): lax.all_to_all(packed, BOTH, split_axis=0, concat_axis=0, tiled=True)  9.29 us
    pallas_call x1, Pallas kernels, patch(): pl.pallas_call(patch_kernel, out_shape=(jax.ShapeDtypeStruct((CX, CY, NZ)...  7.67 us
    all_to_all x1, starting transfers between devices, shards(): lax.all_to_all(packed, BOTH, split_axis=0, concat_axis=0, tiled=True)  6.16 us
    ppermute x6, waiting for transfers between devices, passed_along(): lax.ppermute(value, axis, [(i, (i + by) % peers) for i in range(peers)])  5.38 us
  transfers between devices with their start and end apart: 7, of which 3 were waited for; matrix products, arithmetic and copies ran while one was open for 2% of the time, Pallas kernels for 0%

profile of v1, /device:TPU:0, one launch (start us, length us, event | category | flops | bytes accessed | tf_op | source)
XLA Modules:
  0.0 144.2 jit_solution(6230381522651440203)
XLA Ops:
  0.6 1.4 fusion
  5.9 2.0 %stack.42.meta = s32[8]{0:T(128)} concatenate(s32[1]{0:T(128)} %bitcast.1, s32[1]{0:T(128)} %bitcast.3, s32[1]{0:T(128)} %bitcast.4, s32[2]{0:T(128)} %param.20, s32[2]{0:T(128)} %param.19, s32[1]{0:T(128)} %bitcast.5), dimensions={0} | concatenate | bytes 64 | tf_op jit(solution)/shard_map/stack | solution.py:375
  7.9 47.5 %cheb.1 = (bf16[16,48,2304]{2,1,0:T(8,128)(2,1)}, f32[7,4,56,128]{3,2,1,0:T(8,128)}) custom-call(s32[8]{0:T(128)} %stack.42.meta, bf16[16,48,2304]{2,1,0:T(8,128)(2,1)} %bitcast.41, f32[2,48,2304]{2,1,0:T(8,128)} %pot.1, bf16[128,128]{1,0:T(8,128)(2,1)} %constant.59.clone.eye, bf16[8,128]{1,0:T(8,128)(2,1)} %constant.60.clone.sel), custom_call_target="tpu_custom_call" | custom-call | tf_op jit(solution)/shard_map/cheb/pallas_call | solution.py:186
  55.4 1.2 slice_bitcast_fusion
  56.6 1.6 %collective-permute-start = (f32[4,56,128]{2,1,0:T(8,128)S(1)}, f32[4,56,128]{2,1,0:T(8,128)S(1)}, u32[]{:S(2)}, u32[]{:S(2)}) collective-permute-start(f32[4,56,128]{2,1,0:T(8,128)S(1)} %get-tuple-element.16), channel_id=1, source_target_pairs={{0,1},{1,2},{2,3},{3,4},{4,5},{5,6},{6,7},{7,8},{8,9},{9,10},{10,1... | collective-permute-start | bytes 344072 | tf_op jit(solution)/shard_map/ppermute | solution.py:370
  58.2 2.8 %collective-permute-start.1 = (f32[4,56,128]{2,1,0:T(8,128)S(1)}, f32[4,56,128]{2,1,0:T(8,128)S(1)}, u32[]{:S(2)}, u32[]{:S(2)}) collective-permute-start(f32[4,56,128]{2,1,0:T(8,128)S(1)} %get-tuple-element.15), channel_id=1, source_target_pairs={{0,2},{1,3},{2,4},{3,5},{4,6},{5,7},{6,8},{7,9},{8,10},{9,11},{10,... | collective-permute-start | bytes 344072 | tf_op jit(solution)/shard_map/ppermute | solution.py:370
  61.0 4.0 %collective-permute-start.2 = (f32[4,56,128]{2,1,0:T(8,128)S(1)}, f32[4,56,128]{2,1,0:T(8,128)S(1)}, u32[]{:S(2)}, u32[]{:S(2)}) collective-permute-start(f32[4,56,128]{2,1,0:T(8,128)S(1)} %get-tuple-element.14), channel_id=1, source_target_pairs={{0,3},{1,4},{2,5},{3,6},{4,7},{5,8},{6,9},{7,10},{8,11},{9,12},{10... | collective-permute-start | bytes 344072 | tf_op jit(solution)/shard_map/ppermute | solution.py:370
  65.0 1.7 %collective-permute-start.3 = (f32[4,56,128]{2,1,0:T(8,128)S(1)}, f32[4,56,128]{2,1,0:T(8,128)S(1)}, u32[]{:S(2)}, u32[]{:S(2)}) collective-permute-start(f32[4,56,128]{2,1,0:T(8,128)S(1)} %get-tuple-element.13), channel_id=1, source_target_pairs={{0,4},{1,5},{2,6},{3,7},{4,8},{5,9},{6,10},{7,11},{8,12},{9,13},{1... | collective-permute-start | bytes 344072 | tf_op jit(solution)/shard_map/ppermute | solution.py:370
  66.7 3.2 %collective-permute-start.4 = (f32[4,56,128]{2,1,0:T(8,128)S(1)}, f32[4,56,128]{2,1,0:T(8,128)S(1)}, u32[]{:S(2)}, u32[]{:S(2)}) collective-permute-start(f32[4,56,128]{2,1,0:T(8,128)S(1)} %get-tuple-element.12), channel_id=1, source_target_pairs={{0,5},{1,6},{2,7},{3,8},{4,9},{5,10},{6,11},{7,12},{8,13},{9,14},{... | collective-permute-start | bytes 344072 | tf_op jit(solution)/shard_map/ppermute | solution.py:370
  70.0 0.9 bitcast_dynamic-update-slice_fusion.6
  70.9 0.0 copy-start.1
  70.9 0.0 collective-permute-done
  70.9 4.6 %collective-permute-start.5 = (f32[4,56,128]{2,1,0:T(8,128)S(1)}, f32[4,56,128]{2,1,0:T(8,128)S(1)}, u32[]{:S(2)}, u32[]{:S(2)}) collective-permute-start(f32[4,56,128]{2,1,0:T(8,128)S(1)} %get-tuple-element.11), channel_id=1, source_target_pairs={{0,6},{1,7},{2,8},{3,9},{4,10},{5,11},{6,12},{7,13},{8,14},{9,15},... | collective-permute-start | bytes 344072 | tf_op jit(solution)/shard_map/ppermute | solution.py:370
  75.5 0.0 collective-permute-done.1
  75.6 0.0 collective-permute-done.2
  75.6 4.2 %collective-permute-done.3 = f32[4,56,128]{2,1,0:T(8,128)S(1)} collective-permute-done((f32[4,56,128]{2,1,0:T(8,128)S(1)}, f32[4,56,128]{2,1,0:T(8,128)S(1)}, u32[]{:S(2)}, u32[]{:S(2)}) %collective-permute-start.3) | collective-permute-done | bytes 114720 | tf_op jit(solution)/shard_map/ppermute | solution.py:370
  79.8 0.0 collective-permute-done.4
  79.8 1.2 collective-permute-done.5
  81.0 0.1 copy.20
  81.1 14.9 %all_to_all.27 = f32[4,7,56,128]{3,2,1,0:T(8,128)} all-to-all(f32[4,7,56,128]{3,2,1,0:T(8,128)S(1)} %copy.20), channel_id=1, replica_groups=mesh['row'=4,'col'=32] {'row'}, dimensions={0} | all-to-all | bytes 1605632 | tf_op jit(solution)/shard_map/all_to_all | solution.py:391
  96.0 7.7 %patch.1 = (f32[16,8,512]{2,1,0:T(8,128)}, f32[512,128]{1,0:T(8,128)}) custom-call(f32[28,56,128]{2,1,0:T(8,128)} %bitcast.42, bf16[512,512]{1,0:T(8,128)(2,1)} %constant.61.clone.tab_h, bf16[512,512]{1,0:T(8,128)(2,1)} %constant.62.clone.tab_l), custom_call_target="tpu_custom_call" | custom-call | tf_op jit(solution)/shard_map/patch/pallas_call | solution.py:254
  103.7 6.2 %all-to-all-start.1 = ((f32[128,4,128]{2,1,0:T(4,128)}), f32[128,4,128]{2,1,0:T(4,128)S(1)}, u32[]{:S(2)}, u32[]{:S(2)}) async-start(f32[128,4,128]{2,1,0:T(4,128)} %bitcast.46), calls=%async_computation.1 | async-start | bytes 524288 | tf_op jit(solution)/shard_map/all_to_all | solution.py:395
  109.9 0.7 dynamic-slice_bitcast_fusion
  110.6 0.1 broadcast_in_dim.3
  110.6 0.1 stack_reshape.3
  110.7 0.0 copy-done.1
  110.7 0.6 pad_maximum_fusion.kxz
  111.3 9.3 %all-to-all-done.1 = f32[128,4,128]{2,1,0:T(4,128)S(1)} async-done(((f32[128,4,128]{2,1,0:T(4,128)}), f32[128,4,128]{2,1,0:T(4,128)S(1)}, u32[]{:S(2)}, u32[]{:S(2)}) %all-to-all-start.1) | async-done | bytes 262176 | tf_op jit(solution)/shard_map/all_to_all | solution.py:395
  120.6 0.7 copy-done
  121.3 4.0 %middle.1 = f32[512,128]{1,0:T(8,128)} custom-call(f32[512,128]{1,0:T(8,128)} %bitcast.43, f32[2,256]{1,0:T(2,128)} %pad_maximum_fusion.kxz, f32[256,1]{1,0:T(8,128)} %constant.65.clone.ky, bf16[2,512,128]{2,1,0:T(8,128)(2,1)} %constant.66.clone.ry, bf16[2,256,256]{2,1,0:T(8,128)(2,1)} %constant.67.clone.ryt, bf16[2,512,256]{2,1,0:T(8,128)(2,1)} %constant.68.clone.bx, ...), custom_call_target="tpu_custom_call" | custom-call | tf_op jit(solution)/shard_map/middle/pallas_call | solution.py:285
  125.3 16.2 %all_to_all.28 = f32[128,4,128]{2,1,0:T(4,128)} all-to-all(f32[128,4,128]{2,1,0:T(4,128)} %bitcast.44), channel_id=1, replica_groups=mesh['row'=4,'col'=32] {'row','col'}, dimensions={0} | all-to-all | bytes 524288 | tf_op jit(solution)/shard_map/all_to_all | solution.py:400
  141.5 2.7 %final.1 = f32[16,8,512]{2,1,0:T(8,128)} custom-call(f32[512,128]{1,0:T(8,128)} %bitcast.45, bf16[512,512]{1,0:T(8,128)(2,1)} %constant.61.clone.tab_h, bf16[512,512]{1,0:T(8,128)(2,1)} %constant.62.clone.tab_l), custom_call_target="tpu_custom_call" | custom-call | tf_op jit(solution)/shard_map/final/pallas_call | solution.py:315
  (7 shorter events, 0.1 us)
Async XLA Ops:
  56.6 14.3 %collective-permute-start = (f32[4,56,128]{2,1,0:T(8,128)S(1)}, f32[4,56,128]{2,1,0:T(8,128)S(1)}, u32[]{:S(2)}, u32[]{:S(2)}) collective-permute-start(f32[4,56,128]{2,1,0:T(8,128)S(1)} %get-tuple-element.16), channel_id=1, source_target_pairs={{0,1},{1,2},{2,3},{3,4},{4,5},{5,6},{6,7},{7,8},{8,9},{9,10},{10,1... | collective-permute-start | bytes 344072 | tf_op jit(solution)/shard_map/ppermute | solution.py:370
  58.2 17.3 %collective-permute-start.1 = (f32[4,56,128]{2,1,0:T(8,128)S(1)}, f32[4,56,128]{2,1,0:T(8,128)S(1)}, u32[]{:S(2)}, u32[]{:S(2)}) collective-permute-start(f32[4,56,128]{2,1,0:T(8,128)S(1)} %get-tuple-element.15), channel_id=1, source_target_pairs={{0,2},{1,3},{2,4},{3,5},{4,6},{5,7},{6,8},{7,9},{8,10},{9,11},{10,... | collective-permute-start | bytes 344072 | tf_op jit(solution)/shard_map/ppermute | solution.py:370
  61.0 14.6 %collective-permute-start.2 = (f32[4,56,128]{2,1,0:T(8,128)S(1)}, f32[4,56,128]{2,1,0:T(8,128)S(1)}, u32[]{:S(2)}, u32[]{:S(2)}) collective-permute-start(f32[4,56,128]{2,1,0:T(8,128)S(1)} %get-tuple-element.14), channel_id=1, source_target_pairs={{0,3},{1,4},{2,5},{3,6},{4,7},{5,8},{6,9},{7,10},{8,11},{9,12},{10... | collective-permute-start | bytes 344072 | tf_op jit(solution)/shard_map/ppermute | solution.py:370
  65.0 14.8 %collective-permute-start.3 = (f32[4,56,128]{2,1,0:T(8,128)S(1)}, f32[4,56,128]{2,1,0:T(8,128)S(1)}, u32[]{:S(2)}, u32[]{:S(2)}) collective-permute-start(f32[4,56,128]{2,1,0:T(8,128)S(1)} %get-tuple-element.13), channel_id=1, source_target_pairs={{0,4},{1,5},{2,6},{3,7},{4,8},{5,9},{6,10},{7,11},{8,12},{9,13},{1... | collective-permute-start | bytes 344072 | tf_op jit(solution)/shard_map/ppermute | solution.py:370
  66.7 13.0 %collective-permute-start.4 = (f32[4,56,128]{2,1,0:T(8,128)S(1)}, f32[4,56,128]{2,1,0:T(8,128)S(1)}, u32[]{:S(2)}, u32[]{:S(2)}) collective-permute-start(f32[4,56,128]{2,1,0:T(8,128)S(1)} %get-tuple-element.12), channel_id=1, source_target_pairs={{0,5},{1,6},{2,7},{3,8},{4,9},{5,10},{6,11},{7,12},{8,13},{9,14},{... | collective-permute-start | bytes 344072 | tf_op jit(solution)/shard_map/ppermute | solution.py:370
  70.9 39.8 %copy-start.1 = (f32[1,256]{1,0:T(1,128)S(1)}, f32[1,256]{1,0:T(1,128)}, u32[]{:S(2)}) copy-start(f32[1,256]{1,0:T(1,128)} %constant.75) | copy-start | bytes 3076
  70.9 10.1 %collective-permute-start.5 = (f32[4,56,128]{2,1,0:T(8,128)S(1)}, f32[4,56,128]{2,1,0:T(8,128)S(1)}, u32[]{:S(2)}, u32[]{:S(2)}) collective-permute-start(f32[4,56,128]{2,1,0:T(8,128)S(1)} %get-tuple-element.11), channel_id=1, source_target_pairs={{0,6},{1,7},{2,8},{3,9},{4,10},{5,11},{6,12},{7,13},{8,14},{9,15},... | collective-permute-start | bytes 344072 | tf_op jit(solution)/shard_map/ppermute | solution.py:370
  103.7 16.9 %all-to-all-start.1 = ((f32[128,4,128]{2,1,0:T(4,128)}), f32[128,4,128]{2,1,0:T(4,128)S(1)}, u32[]{:S(2)}, u32[]{:S(2)}) async-start(f32[128,4,128]{2,1,0:T(4,128)} %bitcast.46), calls=%async_computation.1 | async-start | bytes 524288 | tf_op jit(solution)/shard_map/all_to_all | solution.py:395
  120.6 0.7 copy-start
